TPU v7x, 32 devices: a whole 2x2x4 slice. The times are simulated.
32 devices in a mesh: req: 8 (over y, x, core), mp: 4 (over z).
Axes of the slice: x: 2, y: 2, z: 4, core: 2. Of those that a mesh axis runs over, the one named last changes fastest.
Arguments:
- latents: bfloat16 [16, 1, 384, 416], P('req', None, 'mp'), may hold values from -12 to 12
- prior_frame_cache: bfloat16 [16, 2, 384, 416], P('req', None, 'mp'), may hold values from -6 to 6
- move_to: int32 [16], P('req'), may hold values from 0 to 15, as said below
- counts: int32 [8], P('req'), may hold values from 1 to 2, as said below
- norm_gain: bfloat16 [384], P('mp'), may hold values from 0.5 to 1.5
- conv_weight: bfloat16 [27, 384, 384], P(None, 'mp'), may hold values from -0.0625 to 0.0625
- conv_bias: float32 [384], P('mp'), may hold values from -1.5 to 1.5
Outputs:
- decoded: bfloat16 [16, 1, 384, 416], P('req', None, 'mp')
- new_cache: bfloat16 [16, 2, 384, 416], P('req', None, 'mp')
Inputs may be any that keep to these rules, and one draw needn't show every extreme that they name: move_to is a permutation of the slots; a stream's new slot lies on its old index of req or on the next or previous one, the last and first index being neighbours; every index hands exactly 1 stream to each neighbour and takes the same number back from it. `counts`: some index of req is full and some other holds a single stream.
All inputs are finite; a program needn't handle non-finite values.
Results may differ from a plain program's by a relative error of at most 0.0018.
Values may be sent and summed in bfloat16 or wider, within the bound.
A program may use at most 64 MiB of HBM per device.

v0:
```python
import jax
import jax.numpy as jnp
from jax import lax
from jax.sharding import PartitionSpec as P

SECTION_CHANNELS = 384
LATENT_COLUMNS = 104


def shifted_2(block, axis, distance):
    devices = range(lax.axis_size(axis))
    route = [((i - distance) % len(devices), i) for i in devices]
    return lax.ppermute(block, axis, route)


def apply_taps(running, shard_in, weights, row_width):
    frames = shard_in.shape[1] - 2
    pixels = shard_in.shape[3]
    padded = jnp.pad(shard_in, ((0, 0), (0, 0), (0, 0), (row_width + 1, row_width + 1)))
    column = jnp.arange(pixels + 2 * row_width) % row_width
    for step_x in range(3):
        inside = ((column + step_x - 1 >= 0) & (column + step_x - 1 < row_width)).astype(
            shard_in.dtype
        )
        shifted = padded[:, :, :, step_x : step_x + pixels + 2 * row_width] * inside
        for step_y in range(3):
            window = shifted[:, :, :, step_y * row_width : step_y * row_width + pixels]
            for step_t in range(3):
                running = running + jnp.einsum(
                    "oc,stcp->stop",
                    weights[step_t * 9 + step_y * 3 + step_x],
                    window[:, step_t : step_t + frames],
                    preferred_element_type=jnp.float32,
                )
    return running


def pack_slots(prior_frame_cache, chosen, target, capacity):
    ranking = jnp.cumsum(chosen.astype(jnp.int32)) - 1
    picker = (chosen[None, :] & (ranking[None, :] == jnp.arange(capacity)[:, None])).astype(
        jnp.bfloat16
    )
    blocks = jnp.einsum(
        "cs,sfkp->cfkp", picker, prior_frame_cache, preferred_element_type=jnp.float32
    ).astype(jnp.bfloat16)
    labels = (jnp.dot(picker.astype(jnp.float32), (target + 1).astype(jnp.float32)) - 1.0).astype(
        jnp.bfloat16
    )
    return (blocks, labels)


def migrate(prior_frame_cache, move_to):
    slot_count = prior_frame_cache.shape[0]
    member_slots = lax.axis_size("req")
    position = lax.axis_index("req")
    capacity = slot_count // 2
    device = move_to // slot_count
    target = move_to % slot_count
    offset = (device - position) % member_slots
    goes_right = offset == 1
    goes_left = offset == member_slots - 1
    stays_put = offset == 0
    blocks_right, labels_right = pack_slots(prior_frame_cache, goes_right, target, capacity)
    blocks_left, labels_left = pack_slots(prior_frame_cache, goes_left, target, capacity)
    from_left = shifted_2((blocks_right, labels_right), "req", 1)
    from_right = shifted_2((blocks_left, labels_left), "req", -1)
    sources = jnp.concatenate([prior_frame_cache, from_left[0], from_right[0]], axis=0)
    own_labels = jnp.where(stays_put, target, -1).astype(jnp.float32)
    labels = jnp.concatenate(
        [own_labels, from_left[1].astype(jnp.float32), from_right[1].astype(jnp.float32)]
    )
    placing = (labels[None, :] == jnp.arange(slot_count, dtype=jnp.float32)[:, None]).astype(
        jnp.bfloat16
    )
    return jnp.einsum("ns,sfkp->nfkp", placing, sources, preferred_element_type=jnp.float32).astype(
        jnp.bfloat16
    )


def normalize(values, squares, gains):
    scaled = (
        values.astype(jnp.float32)
        * lax.rsqrt(squares / SECTION_CHANNELS + 1e-06)
        * gains.astype(jnp.float32)[:, None]
    )
    return jax.nn.silu(scaled).astype(jnp.bfloat16)


def shards(latents, prior_frame_cache, move_to, counts, norm_gain, conv_weight, conv_bias):
    moved = migrate(prior_frame_cache, move_to)
    slot_count = latents.shape[0]
    frames = latents.shape[1]
    live = (jnp.arange(slot_count) < counts[0])[:, None, None, None]
    start_zero = jnp.zeros(
        (slot_count, frames, conv_weight.shape[1], latents.shape[3]), jnp.float32
    )
    values = latents.astype(jnp.float32)
    partial_squares = jnp.sum(values * values, axis=2, keepdims=True)
    squares = lax.psum(partial_squares, "mp")
    hidden = normalize(latents, squares, norm_gain)
    extended = jnp.concatenate([moved, hidden], axis=1)
    conv_sum = apply_taps(
        start_zero, lax.all_gather(extended, "mp", axis=2, tiled=True), conv_weight, LATENT_COLUMNS
    )
    total = latents.astype(jnp.float32) + conv_sum + conv_bias[:, None]
    decoded = jnp.where(live, total, jnp.zeros_like(total)).astype(jnp.bfloat16)
    new_cache = extended[:, frames:]
    return (decoded, new_cache)


def solution(mesh):
    in_specs = (
        P("req", None, "mp", None),
        P("req", None, "mp", None),
        P("req"),
        P("req"),
        P("mp"),
        P(None, "mp", None),
        P("mp"),
    )
    out_specs = (P("req", None, "mp", None), P("req", None, "mp", None))
    return jax.shard_map(shards, mesh=mesh, in_specs=in_specs, out_specs=out_specs, check_vma=False)
```

profile of v0, /device:TPU:0, one launch (start us, length us, event | category | flops | bytes accessed | tf_op | source)
XLA Modules:
  0.0 157.5 jit_solution(8122907851598073962)
XLA Ops:
  7.2 0.7 fusion.140
  8.3 0.6 select_reduce_fusion.1
  9.5 1.5 collective-permute-start
  11.7 4.0 %collective-permute-start.1 = (bf16[1]{0:T(256)(128)(2,1)}, bf16[1]{0:T(256)(128)(2,1)}, u32[]{:S(2)}, u32[]{:S(2)}) collective-permute-start(bf16[1]{0:T(256)(128)(2,1)} %bitcast.7), channel_id=1, source_target_pairs={{4,0},{8,4},{12,8},{16,12},{20,16},{24,20},{28,24},{0,28},{5,1},{9... | collective-permute-start | bytes 14 | tf_op jit(solution)/shard_map/ppermute | solution.py:13
  15.7 1.4 copy.130
  17.1 0.6 fusion.135
  17.7 0.3 copy.128
  18.1 0.6 fusion.133
  18.7 0.3 copy.129
  19.0 2.7 %collective-permute-start.3 = (bf16[1,2,96,416]{3,0,2,1:T(2,128)(2,1)S(1)}, bf16[1,2,96,416]{3,0,2,1:T(2,128)(2,1)S(1)}, u32[]{:S(2)}, u32[]{:S(2)}) collective-permute-start(bf16[1,2,96,416]{3,0,2,1:T(2,128)(2,1)S(1)} %copy.129), channel_id=1, source_target_pairs={{4,0},{8,4},{12,8},{16,12},{20,16},{24,20},{28,24},{0,28},{5,1},{9... | collective-permute-start | bytes 479240 | tf_op jit(solution)/shard_map/ppermute | solution.py:13
  21.7 12.7 %psum.7 = f32[2,1,1,416]{3,0,2,1:T(2,128)S(1)} all-reduce(f32[2,1,1,416]{3,0,2,1:T(2,128)S(1)} %bitcast.336), channel_id=1, replica_groups=mesh['req'=8,'mp'=4] {'mp'}, use_global_device_ids=true, to_apply=%region_3.4 | all-reduce | flops 832 | bytes 6656 | tf_op jit(solution)/shard_map/psum | solution.py:99
  36.3 1.5 convolution_convert_fusion
  37.8 1.7 %pad_maximum_fusion.2 = bf16[2,3,96,416]{3,0,2,1:T(2,128)(2,1)} fusion(bf16[2,1,96,416]{3,0,2,1:T(2,128)(2,1)S(1)} %copy.131, bf16[2,2,96,416]{3,0,2,1:T(2,128)(2,1)S(1)} %convolution_convert_fusion), kind=kLoop, calls=%fused_computation.110 | loop fusion | flops 239616 | bytes 958464 | tf_op jit(solution)/shard_map/concatenate | solution.py:101
  40.2 0.6 fusion.49
  40.8 0.8 copy.160
  41.6 45.3 %all-gather.2.cloned.1.call-done = bf16[2,3,384,416]{3,0,2,1:T(2,128)(2,1)} async-done(((bf16[2,3,96,416]{3,0,2,1:T(2,128)(2,1)}), bf16[2,3,384,416]{3,0,2,1:T(2,128)(2,1)}) %all-gather.2.cloned.1.call-update) | async-done | bytes 1916944 | tf_op jit(solution)/shard_map/all_gather | solution.py:103
  87.0 18.8 %slice_multiply_fusion.2 = (bf16[2,3,384,624]{3,0,2,1:T(2,128)(2,1)S(1)}, bf16[2,3,384,624]{3,0,2,1:T(2,128)(2,1)S(1)}, bf16[2,3,384,624]{3,0,2,1:T(2,128)(2,1)S(1)}) fusion(bf16[624]{0:T(1024)(128)(2,1)S(1)} %fusion.127, bf16[2,3,384,416]{3,0,2,1:T(2,128)(2,1)} %all-gather.2.cloned.1.call-done, bf16[624]{0:T(1024)(128)(2,1)S(1)} %fusion.129, ...), kind=kLoop, calls=%fused_computation.2 | loop fusion | flops 17252352 | bytes 10546848 | tf_op jit(solution)/shard_map/mul | solution.py:25
  105.8 10.7 %slice_bitcast_fusion.18 = (bf16[2,384,416]{2,0,1:T(2,128)(2,1)S(1)}, bf16[2,384,416]{2,0,1:T(2,128)(2,1)S(1)}, bf16[2,384,416]{2,0,1:T(2,128)(2,1)S(1)}, bf16[2...) fusion(bf16[2,3,384,624]{3,0,2,1:T(2,128)(2,1)S(1)} %get-tuple-, ...), kind=kLoop, calls=%fused_computation.66 | loop fusion | bytes 11501568 | tf_op jit(solution)/shard_map/reshape.33
  116.8 25.4 %slice_bitcast_fusion.8 = (bf16[2,384,416]{2,0,1:T(2,128)(2,1)S(1)}, bf16[2,384,416]{2,0,1:T(2,128)(2,1)S(1)}, bf16[2,384,416]{2,0,1:T(2,128)(2,1)S(1)}, bf16[2,...) fusion(bf16[2,3,384,624]{3,0,2,1:T(2,128)(2,1)S(1)} %get-tuple-, ...), kind=kLoop, calls=%fused_computation.56 | loop fusion | bytes 23003136 | tf_op jit(solution)/shard_map/reshape.53
  145.4 0.3 convolution_add_fusion.13
  145.7 0.3 convolution_add_fusion.12
  145.9 0.3 convolution_add_fusion.11
  146.2 0.3 convolution_add_fusion.10
  146.5 0.3 convolution_add_fusion.9
  146.8 0.3 convolution_add_fusion.8
  147.1 0.3 convolution_add_fusion.7
  147.4 0.3 convolution_add_fusion.6
  147.7 0.3 convolution_add_fusion.5
  148.0 0.3 convolution_add_fusion.4
  148.3 0.3 convolution_add_fusion.3
  148.6 0.3 convolution_add_fusion.2
  149.6 1.1 fusion.17
  (44 shorter events, 5.2 us)
Async XLA Ops:
  7.2 79.8 %all-gather.2.cloned.1.call-start = ((), (), s32[]{:S(2)}) async-start(), calls=%async_computation | async-start | bytes 2949120 | tf_op jit(solution)/shard_map/all_gather | solution.py:103
  9.5 25.4 %collective-permute-start = (bf16[1]{0:T(256)(128)(2,1)}, bf16[1]{0:T(256)(128)(2,1)}, u32[]{:S(2)}, u32[]{:S(2)}) collective-permute-start(bf16[1]{0:T(256)(128)(2,1)} %bitcast.4), channel_id=1, source_target_pairs={{28,0},{0,4},{4,8},{8,12},{12,16},{16,20},{20,24},{24,28},{29,1},{... | collective-permute-start | bytes 14 | tf_op jit(solution)/shard_map/ppermute | solution.py:13
  11.7 23.9 %collective-permute-start.1 = (bf16[1]{0:T(256)(128)(2,1)}, bf16[1]{0:T(256)(128)(2,1)}, u32[]{:S(2)}, u32[]{:S(2)}) collective-permute-start(bf16[1]{0:T(256)(128)(2,1)} %bitcast.7), channel_id=1, source_target_pairs={{4,0},{8,4},{12,8},{16,12},{20,16},{24,20},{28,24},{0,28},{5,1},{9... | collective-permute-start | bytes 14 | tf_op jit(solution)/shard_map/ppermute | solution.py:13
  17.6 4.0 %copy-start.3 = (bf16[96]{0:T(256)(128)(2,1)S(1)}, bf16[96]{0:T(256)(128)(2,1)}, u32[]{:S(2)}) copy-start(bf16[96]{0:T(256)(128)(2,1)} %param.11) | copy-start | bytes 580
  17.6 4.0 %copy-start.1 = (bf16[2,1,96,416]{3,2,1,0:T(8,128)(2,1)S(1)}, bf16[2,1,96,416]{3,2,1,0:T(8,128)(2,1)}, u32[]{:S(2)}) copy-start(bf16[2,1,96,416]{3,2,1,0:T(8,128)(2,1)} %param.7) | copy-start | bytes 479236
  18.0 18.3 %collective-permute-start.2 = (bf16[1,2,96,416]{3,0,2,1:T(2,128)(2,1)S(1)}, bf16[1,2,96,416]{3,0,2,1:T(2,128)(2,1)S(1)}, u32[]{:S(2)}, u32[]{:S(2)}) collective-permute-start(bf16[1,2,96,416]{3,0,2,1:T(2,128)(2,1)S(1)} %copy.128), channel_id=1, source_target_pairs={{28,0},{0,4},{4,8},{8,12},{12,16},{16,20},{20,24},{24,28},{29,1},{... | collective-permute-start | bytes 479240 | tf_op jit(solution)/shard_map/ppermute | solution.py:13
  19.0 17.3 %collective-permute-start.3 = (bf16[1,2,96,416]{3,0,2,1:T(2,128)(2,1)S(1)}, bf16[1,2,96,416]{3,0,2,1:T(2,128)(2,1)S(1)}, u32[]{:S(2)}, u32[]{:S(2)}) collective-permute-start(bf16[1,2,96,416]{3,0,2,1:T(2,128)(2,1)S(1)} %copy.129), channel_id=1, source_target_pairs={{4,0},{8,4},{12,8},{16,12},{20,16},{24,20},{28,24},{0,28},{5,1},{9... | collective-permute-start | bytes 479240 | tf_op jit(solution)/shard_map/ppermute | solution.py:13
  105.8 10.7 %copy-start = (bf16[27,96,384]{2,1,0:T(8,128)(2,1)S(1)}, bf16[27,96,384]{2,1,0:T(8,128)(2,1)}, u32[]{:S(2)}) copy-start(bf16[27,96,384]{2,1,0:T(8,128)(2,1)} %param.12) | copy-start | bytes 5971972
  148.9 0.7 copy-start.2
Sparse Core Ops, SparseCore 0:
  39.7 47.2 all-gather.1
where the time goes:
time: 158 us
  waiting for transfers between devices  45.3 us (29%)
  local copies, waits for them, and re-layouts  39.2 us (25%)
  other arithmetic  23.1 us (15%)
  between operations  17.7 us (11%)
  blocking collectives  12.7 us (8%)
  matrix products  11.2 us (7%)
  starting transfers between devices  8.27 us (5%)
    all_gather x1, waiting for transfers between devices, shards(): lax.all_gather(extended, 'mp', axis=2, tiled=True)  45.3 us
    another operation x2, local copies, waits for them, and re-layouts  36.1 us
    mul x1, other arithmetic, apply_taps(): shifted = padded[:, :, :, step_x:step_x + pixels + 2 * row_width] * inside  18.8 us
    psum x1, blocking collectives, shards(): squares = lax.psum(partial_squares, 'mp')  12.7 us
    dot_general x27, matrix products, apply_taps(): jnp.einsum('oc,stcp->stop', weights[step_t * 9 + step_y * 3 + step_x], wi...  8.54 us
    ppermute x4, starting transfers between devices, shifted_2(): return lax.ppermute(block, axis, route)  8.23 us
  transfers between devices with their start and end apart: 5, of which 1 were waited for; matrix products, arithmetic and copies ran while one was open for 3% of the time, Pallas kernels for 0%

commit v1 on v0

--- a/solution.py
+++ b/solution.py
@@ -1,6 +1,10 @@
+import functools
+
 import jax
 import jax.numpy as jnp
 from jax import lax
+from jax.experimental import pallas as pl
+from jax.experimental.pallas import tpu as pltpu
 from jax.sharding import PartitionSpec as P
 
 SECTION_CHANNELS = 384
@@ -86,7 +90,7 @@
     return jax.nn.silu(scaled).astype(jnp.bfloat16)
 
 
-def shards(latents, prior_frame_cache, move_to, counts, norm_gain, conv_weight, conv_bias):
+def shards_plain(latents, prior_frame_cache, move_to, counts, norm_gain, conv_weight, conv_bias):
     moved = migrate(prior_frame_cache, move_to)
     slot_count = latents.shape[0]
     frames = latents.shape[1]
@@ -106,6 +110,316 @@
     decoded = jnp.where(live, total, jnp.zeros_like(total)).astype(jnp.bfloat16)
     new_cache = extended[:, frames:]
     return (decoded, new_cache)
+
+
+MESH = pl.DeviceIdType.MESH
+
+
+def lane_pad(n):
+    return (n + 127) // 128 * 128
+
+
+def column_of(row):
+    n = row.shape[1]
+    square = lax.broadcasted_iota(jnp.int32, (n, n), 0) == lax.broadcasted_iota(
+        jnp.int32, (n, n), 1
+    )
+    return jnp.sum(jnp.where(square, jnp.broadcast_to(row, (n, n)), 0.0), axis=1, keepdims=True)
+
+
+def pack_pair(first, second, extra, packed):
+    rows, pixels = first.shape
+    tail = jnp.broadcast_to(extra, (rows, packed - 2 * pixels))
+    return jnp.concatenate([first, second, tail], axis=1)
+
+
+def second_half(pair, pixels, wide):
+    start = pixels // 128 * 128
+    part = pair[:, start : start + wide].astype(jnp.float32)
+    return pltpu.roll(part, wide - pixels % 128, axis=1).astype(jnp.bfloat16)
+
+
+def block_kernel(
+    n,
+    ring,
+    row_width,
+    move_ref,
+    counts_ref,
+    lat_ref,
+    cache_ref,
+    gain_ref,
+    bias_ref,
+    w_ref,
+    dec_ref,
+    new_ref,
+    wcat,
+    gath,
+    mig_out,
+    mig_in,
+    stack,
+    acc,
+    w_sem,
+    mig_send,
+    mig_recv,
+    up_send,
+    down_send,
+    ag_recv,
+):
+    me = lax.axis_index("mp")
+    pos = lax.axis_index("req")
+    rows, pixels = lat_ref.shape[2], lat_ref.shape[3]
+    packed = gath.shape[3]
+    wide = stack.shape[2]
+    channels = n * rows
+    right, left = lax.rem(pos + 1, ring), lax.rem(pos + ring - 1, ring)
+
+    w_copies = []
+    for kt in range(3):
+        copy = pltpu.make_async_copy(
+            w_ref.at[pl.ds(9 * kt, 9)],
+            wcat.at[:, :, pl.ds(channels * kt, channels)],
+            w_sem.at[kt],
+        )
+        copy.start()
+        w_copies.append(copy)
+
+    barrier = pltpu.get_barrier_semaphore()
+    for neighbour in (right, left):
+        pl.semaphore_signal(barrier, inc=1, device_id={"req": neighbour}, device_id_type=MESH)
+
+    @pl.when(me < n - 1)
+    def _():
+        pl.semaphore_signal(barrier, inc=1, device_id={"mp": me + 1}, device_id_type=MESH)
+
+    @pl.when(me > 0)
+    def _():
+        pl.semaphore_signal(barrier, inc=1, device_id={"mp": me - 1}, device_id_type=MESH)
+
+    gain = column_of(gain_ref[...].astype(jnp.float32))
+    gath[0, me] = pack_pair(
+        lat_ref[0, 0].astype(jnp.float32), lat_ref[1, 0].astype(jnp.float32), gain, packed
+    ).astype(jnp.bfloat16)
+
+    inner = (me > 0) & (me < n - 1)
+
+    @pl.when(inner)
+    def _():
+        pl.semaphore_wait(barrier, 4)
+
+    @pl.when(jnp.logical_not(inner))
+    def _():
+        pl.semaphore_wait(barrier, 3)
+
+    def up_copy(j, src):
+        return pltpu.make_async_remote_copy(
+            src_ref=gath.at[j, src],
+            dst_ref=gath.at[j, src],
+            send_sem=up_send.at[j, src],
+            recv_sem=ag_recv.at[j, src],
+            device_id={"mp": me + 1},
+            device_id_type=MESH,
+        )
+
+    def down_copy(j, src):
+        return pltpu.make_async_remote_copy(
+            src_ref=gath.at[j, src],
+            dst_ref=gath.at[j, src],
+            send_sem=down_send.at[j, src],
+            recv_sem=ag_recv.at[j, src],
+            device_id={"mp": me - 1},
+            device_id_type=MESH,
+        )
+
+    def send_own(j):
+        @pl.when(me < n - 1)
+        def _():
+            up_copy(j, me).start()
+
+        @pl.when(me > 0)
+        def _():
+            down_copy(j, me).start()
+
+    def relay(j, d):
+        @pl.when(me - d >= 0)
+        def _():
+            down_copy(j, me - d).wait_recv()
+
+            @pl.when(me < n - 1)
+            def _():
+                up_copy(j, me - d).start()
+
+        @pl.when(me + d <= n - 1)
+        def _():
+            up_copy(j, me + d).wait_recv()
+
+            @pl.when(me > 0)
+            def _():
+                down_copy(j, me + d).start()
+
+    send_own(0)
+
+    slots = lat_ref.shape[0]
+    offset = lax.rem(lax.div(move_ref[0], slots) - pos + ring, ring)
+    first_right = jnp.where(offset == 1, 1.0, 0.0).astype(jnp.float32)
+    pairs = []
+    for s in range(2):
+        label = jnp.full((rows, 1), lax.rem(move_ref[s], slots), jnp.int32).astype(jnp.float32)
+        pairs.append(
+            pack_pair(
+                cache_ref[s, 0].astype(jnp.float32),
+                cache_ref[s, 1].astype(jnp.float32),
+                label,
+                packed,
+            )
+        )
+    pick = jnp.full((rows, packed), first_right, jnp.float32) > 0.5
+    mig_out[0] = jnp.where(pick, pairs[0], pairs[1]).astype(jnp.bfloat16)
+    mig_out[1] = jnp.where(pick, pairs[1], pairs[0]).astype(jnp.bfloat16)
+    moves = []
+    for k, neighbour in enumerate((right, left)):
+        copy = pltpu.make_async_remote_copy(
+            src_ref=mig_out.at[k],
+            dst_ref=mig_in.at[k],
+            send_sem=mig_send.at[k],
+            recv_sem=mig_recv.at[k],
+            device_id={"req": neighbour},
+            device_id_type=MESH,
+        )
+        copy.start()
+        moves.append(copy)
+
+    relay(0, 1)
+    for copy in moves:
+        copy.wait_recv()
+    from_left = mig_in[0].astype(jnp.float32)
+    from_right = mig_in[1].astype(jnp.float32)
+    to_second = jnp.broadcast_to(from_left[:, 2 * pixels : 2 * pixels + 1], (rows, packed)) > 0.5
+    gath[1, me] = jnp.where(to_second, from_right, from_left).astype(jnp.bfloat16)
+    gath[2, me] = jnp.where(to_second, from_left, from_right).astype(jnp.bfloat16)
+    send_own(1)
+    send_own(2)
+    for d in range(2, n):
+        relay(0, d)
+
+    own = pl.multiple_of(me * rows, rows)
+    values = gath[0].reshape(channels, packed).astype(jnp.float32)
+    gains = values[:, 2 * pixels : 2 * pixels + 1]
+    squares = jnp.sum(values * values, axis=0, keepdims=True)
+    scaled = values * lax.rsqrt(squares / channels + 1e-06) * gains
+    hidden = (scaled / (1.0 + jnp.exp(-scaled))).astype(jnp.bfloat16)
+    stack[0, pl.ds(2 * channels, channels)] = hidden[:, :wide]
+    stack[1, pl.ds(2 * channels, channels)] = second_half(hidden, pixels, wide)
+    for copy in w_copies:
+        copy.wait()
+    taps = 9 * rows
+    for s in range(2):
+        new_ref[s, 1] = stack[s, pl.ds(2 * channels + own, rows), :pixels]
+        acc[s] = jnp.dot(
+            wcat[:, :, 2 * channels :].reshape(taps, channels),
+            stack[s, pl.ds(2 * channels, channels)],
+            preferred_element_type=jnp.float32,
+        )
+
+    for d in range(1, n - 1):
+        relay(1, d)
+        relay(2, d)
+
+    lane = lax.broadcasted_iota(jnp.int32, (1, wide), 1)
+    column = lax.rem(lane, row_width)
+    bias = column_of(bias_ref[...])
+    for s in range(2):
+        relay(1 + s, n - 1)
+        pair = gath[1 + s].reshape(channels, packed)
+        stack[s, :channels] = pair[:, :wide]
+        stack[s, pl.ds(channels, channels)] = second_half(pair, pixels, wide)
+        new_ref[s, 0] = stack[s, pl.ds(channels + own, rows), :pixels]
+        acc[s] += jnp.dot(
+            wcat[:, :, : 2 * channels].reshape(taps, 2 * channels),
+            stack[s, : 2 * channels],
+            preferred_element_type=jnp.float32,
+        )
+        total = jnp.zeros((rows, wide), jnp.float32)
+        for kx in range(3):
+            part = acc[s, pl.ds((3 + kx) * rows, rows)]
+            above = pltpu.roll(acc[s, pl.ds(kx * rows, rows)], row_width, axis=1)
+            part = part + jnp.where(lane >= row_width, above, 0.0)
+            below = pltpu.roll(acc[s, pl.ds((6 + kx) * rows, rows)], wide - row_width, axis=1)
+            part = part + jnp.where(lane < pixels - row_width, below, 0.0)
+            if kx == 0:
+                part = jnp.where(column >= 1, pltpu.roll(part, 1, axis=1), 0.0)
+            if kx == 2:
+                part = jnp.where(column < row_width - 1, pltpu.roll(part, wide - 1, axis=1), 0.0)
+            total = total + part
+        result = lat_ref[s, 0].astype(jnp.float32) + (total + bias)[:, :pixels]
+        live = jnp.full((rows, pixels), counts_ref[0], jnp.int32) > s
+        dec_ref[s, 0] = jnp.where(live, result, 0.0).astype(jnp.bfloat16)
+
+    for copy in moves:
+        copy.wait_send()
+    for j in range(3):
+        for src in range(n):
+            @pl.when((me < n - 1) & (src <= me))
+            def _():
+                up_copy(j, src).wait_send()
+
+            @pl.when((me > 0) & (src >= me))
+            def _():
+                down_copy(j, src).wait_send()
+
+
+def shards_kernel(latents, prior_frame_cache, move_to, counts, norm_gain, conv_weight, conv_bias):
+    n, ring = lax.axis_size("mp"), lax.axis_size("req")
+    rows, pixels = latents.shape[2], latents.shape[3]
+    channels = n * rows
+    packed, wide = lane_pad(2 * pixels + 1), lane_pad(pixels)
+    vmem = pl.BlockSpec(memory_space=pltpu.VMEM)
+    smem = pl.BlockSpec(memory_space=pltpu.SMEM)
+    return pl.pallas_call(
+        functools.partial(block_kernel, n, ring, LATENT_COLUMNS),
+        out_shape=(
+            jax.ShapeDtypeStruct(latents.shape, jnp.bfloat16),
+            jax.ShapeDtypeStruct(prior_frame_cache.shape, jnp.bfloat16),
+        ),
+        in_specs=[smem, smem, vmem, vmem, vmem, vmem, pl.BlockSpec(memory_space=pl.ANY)],
+        out_specs=(vmem, vmem),
+        scratch_shapes=[
+            pltpu.VMEM((9, rows, 3 * channels), jnp.bfloat16),
+            pltpu.VMEM((3, n, rows, packed), jnp.bfloat16),
+            pltpu.VMEM((2, rows, packed), jnp.bfloat16),
+            pltpu.VMEM((2, rows, packed), jnp.bfloat16),
+            pltpu.VMEM((2, 3 * channels, wide), jnp.bfloat16),
+            pltpu.VMEM((2, 9 * rows, wide), jnp.float32),
+            pltpu.SemaphoreType.DMA((3,)),
+            pltpu.SemaphoreType.DMA((2,)),
+            pltpu.SemaphoreType.DMA((2,)),
+            pltpu.SemaphoreType.DMA((3, n)),
+            pltpu.SemaphoreType.DMA((3, n)),
+            pltpu.SemaphoreType.DMA((3, n)),
+        ],
+        compiler_params=pltpu.CompilerParams(
+            collective_id=0, has_side_effects=True, vmem_limit_bytes=56 << 20
+        ),
+    )(
+        move_to,
+        counts,
+        latents,
+        prior_frame_cache,
+        norm_gain.reshape(1, rows),
+        conv_bias.reshape(1, rows),
+        conv_weight,
+    )
+
+
+def shards(latents, *rest):
+    fits = (
+        latents.shape[0] == 2
+        and latents.shape[1] == 1
+        and latents.shape[2] % 32 == 0
+        and lax.axis_size("req") > 2
+        and lax.axis_size("mp") > 1
+        and lax.axis_size("mp") * latents.shape[2] % 128 == 0
+    )
+    return (shards_kernel if fits else shards_plain)(latents, *rest)
 
 
 def solution(mesh):

time: 158 us -> 48.6 us (0.31)
  waiting for transfers between devices: 45.3 us -> 0 us
  Pallas kernels: 0 us -> 43.8 us
  local copies, waits for them, and re-layouts: 39.2 us -> 3.38 us
  other arithmetic: 23.1 us -> 0 us
  between operations: 17.7 us -> 1.29 us
  blocking collectives: 12.7 us -> 0 us
  matrix products: 11.2 us -> 0 us
  starting transfers between devices: 8.27 us -> 0 us
    all_gather x1 -> x0, waiting for transfers between devices: 45.3 us -> none  [shards(): lax.all_gather(extended, 'mp', axis=2, tiled=True)]
    pallas_call x0 -> x1, Pallas kernels: none -> 43.8 us  [shards_kernel(): pl.pallas_call(functools.partial(block_kernel, n, ring, LATENT_COLUMNS),...]
    another operation x2 -> x0, local copies, waits for them, and re-layouts: 36.1 us -> none
    mul x2 -> x0, other arithmetic: 18.8 us -> none  [the longest x1 18.8 us: apply_taps(): shifted = padded[:, :, :, step_x:step_x + pixels + 2 * row_width] * inside]
    psum x1 -> x0, blocking collectives: 12.7 us -> none  [shards(): squares = lax.psum(partial_squares, 'mp')]
    dot_general x30 -> x0, matrix products: 11.2 us -> none  [the longest x27 8.54 us: apply_taps(): jnp.einsum('oc,stcp->stop', weights[step_t * 9 + step_y * 3 + step_x], wi...]
    ppermute x4 -> x0, starting transfers between devices: 8.23 us -> none  [shifted_2(): return lax.ppermute(block, axis, route)]
    concatenate x3 -> x0, other arithmetic: 2.36 us -> none  [the longest x2 2.28 us: shards(): extended = jnp.concatenate([moved, hidden], axis=1)]
  transfers between devices with their start and end apart: 5 -> 0, of which waited for: 1 -> 0; matrix products, arithmetic and copies ran while one was open for 3% -> 0% of each run, Pallas kernels for 0% -> 0%
where the time goes in v1:
time: 48.6 us; the launch traced here: 48.4 us
  Pallas kernels  43.8 us (90%)
  local copies, waits for them, and re-layouts  3.38 us (7%)
  between operations  1.29 us (3%)
    pallas_call x1, Pallas kernels, shards_kernel(): pl.pallas_call(functools.partial(block_kernel, n, ring, LATENT_COLUMNS),...  43.8 us
    unnamed x2, local copies, waits for them, and re-layouts  3.38 us

profile of v1, /device:TPU:0, one launch (start us, length us, event | category | flops | bytes accessed | tf_op | source)
XLA Modules:
  0.0 48.4 jit_solution(9935501718155933628)
XLA Ops:
  1.3 43.8 %shard_map.86 = (bf16[2,1,96,416]{3,2,1,0:T(8,128)(2,1)}, bf16[2,2,96,416]{3,2,1,0:T(8,128)(2,1)}) custom-call(s32[2]{0:T(128)} %move_ref.1, s32[1]{0:T(128)S(6)} %copy.11.counts_ref, bf16[2,1,96,416]{3,2,1,0:T(8,128)(2,1)} %lat_ref.1, bf16[2,2,96,416]{3,2,1,0:T(8,128)(2,1)} %cache_ref.1, bf16[1,96]{1,0:T(2,128)(2,1)} %bitcast.2, f32[1,96]{1,0:T(1,128)} %bitcast.3, ...), custom_call_target="tpu_custom_call" | custom-call | tf_op jit(solution)/shard_map/pallas_call | solution.py:377
  45.0 1.6 %copy.12 = bf16[2,1,96,416]{3,2,1,0:T(8,128)(2,1)} copy(bf16[2,1,96,416]{3,2,1,0:T(8,128)(2,1)} %get-tuple-element.4) | data formatting | bytes 319488
  46.7 1.8 %copy.13 = bf16[2,2,96,416]{3,2,1,0:T(8,128)(2,1)} copy(bf16[2,2,96,416]{3,2,1,0:T(8,128)(2,1)} %get-tuple-element.5) | data formatting | bytes 638976

commit v2 on v1

--- a/solution.py
+++ b/solution.py
@@ -154,6 +154,7 @@
     new_ref,
     wcat,
     gath,
+    last,
     mig_out,
     mig_in,
     stack,
@@ -210,10 +211,17 @@
     def _():
         pl.semaphore_wait(barrier, 3)
 
+    half = rows // 2
+
+    def piece(j, src):
+        if j < 2:
+            return gath.at[0, src, pl.ds(half * j, half)]
+        return gath.at[1, src] if j == 2 else last.at[src]
+
     def up_copy(j, src):
         return pltpu.make_async_remote_copy(
-            src_ref=gath.at[j, src],
-            dst_ref=gath.at[j, src],
+            src_ref=piece(j, src),
+            dst_ref=piece(j, src),
             send_sem=up_send.at[j, src],
             recv_sem=ag_recv.at[j, src],
             device_id={"mp": me + 1},
@@ -222,8 +230,8 @@
 
     def down_copy(j, src):
         return pltpu.make_async_remote_copy(
-            src_ref=gath.at[j, src],
-            dst_ref=gath.at[j, src],
+            src_ref=piece(j, src),
+            dst_ref=piece(j, src),
             send_sem=down_send.at[j, src],
             recv_sem=ag_recv.at[j, src],
             device_id={"mp": me - 1},
@@ -257,6 +265,7 @@
                 down_copy(j, me + d).start()
 
     send_own(0)
+    send_own(1)
 
     slots = lat_ref.shape[0]
     offset = lax.rem(lax.div(move_ref[0], slots) - pos + ring, ring)
@@ -289,17 +298,24 @@
         moves.append(copy)
 
     relay(0, 1)
+    relay(1, 1)
     for copy in moves:
         copy.wait_recv()
     from_left = mig_in[0].astype(jnp.float32)
     from_right = mig_in[1].astype(jnp.float32)
     to_second = jnp.broadcast_to(from_left[:, 2 * pixels : 2 * pixels + 1], (rows, packed)) > 0.5
-    gath[1, me] = jnp.where(to_second, from_right, from_left).astype(jnp.bfloat16)
-    gath[2, me] = jnp.where(to_second, from_left, from_right).astype(jnp.bfloat16)
-    send_own(1)
+    slot_0 = jnp.where(to_second, from_right, from_left)
+    slot_1 = jnp.where(to_second, from_left, from_right)
+    spill = packed - 2 * pixels
+    turned = pltpu.roll(slot_1, packed - spill, axis=1)
+    spare = lax.broadcasted_iota(jnp.int32, (rows, packed), 1) >= 2 * pixels
+    gath[1, me] = jnp.where(spare, turned, slot_0).astype(jnp.bfloat16)
+    last[me] = turned[:, : packed - 128].astype(jnp.bfloat16)
     send_own(2)
+    send_own(3)
     for d in range(2, n):
         relay(0, d)
+        relay(1, d)
 
     own = pl.multiple_of(me * rows, rows)
     values = gath[0].reshape(channels, packed).astype(jnp.float32)
@@ -321,15 +337,20 @@
         )
 
     for d in range(1, n - 1):
-        relay(1, d)
         relay(2, d)
+        relay(3, d)
 
     lane = lax.broadcasted_iota(jnp.int32, (1, wide), 1)
     column = lax.rem(lane, row_width)
     bias = column_of(bias_ref[...])
     for s in range(2):
-        relay(1 + s, n - 1)
-        pair = gath[1 + s].reshape(channels, packed)
+        relay(2 + s, n - 1)
+        pair = gath[1].reshape(channels, packed)
+        if s == 1:
+            rest = last[...].reshape(channels, packed - 128).astype(jnp.float32)
+            head = pair[:, packed - 128 :].astype(jnp.float32)
+            pair = jnp.concatenate([rest, head], axis=1)
+            pair = pltpu.roll(pair, spill, axis=1).astype(jnp.bfloat16)
         stack[s, :channels] = pair[:, :wide]
         stack[s, pl.ds(channels, channels)] = second_half(pair, pixels, wide)
         new_ref[s, 0] = stack[s, pl.ds(channels + own, rows), :pixels]
@@ -356,7 +377,7 @@
 
     for copy in moves:
         copy.wait_send()
-    for j in range(3):
+    for j in range(4):
         for src in range(n):
             @pl.when((me < n - 1) & (src <= me))
             def _():
@@ -365,6 +386,11 @@
             @pl.when((me > 0) & (src >= me))
             def _():
                 down_copy(j, src).wait_send()
+
+
+def place_kernel(dec_ref, new_ref, dec_out, new_out):
+    dec_out[...] = dec_ref[...]
+    new_out[...] = new_ref[...]
 
 
 def shards_kernel(latents, prior_frame_cache, move_to, counts, norm_gain, conv_weight, conv_bias):
@@ -374,17 +400,18 @@
     packed, wide = lane_pad(2 * pixels + 1), lane_pad(pixels)
     vmem = pl.BlockSpec(memory_space=pltpu.VMEM)
     smem = pl.BlockSpec(memory_space=pltpu.SMEM)
-    return pl.pallas_call(
+    results = pl.pallas_call(
         functools.partial(block_kernel, n, ring, LATENT_COLUMNS),
         out_shape=(
             jax.ShapeDtypeStruct(latents.shape, jnp.bfloat16),
             jax.ShapeDtypeStruct(prior_frame_cache.shape, jnp.bfloat16),
         ),
-        in_specs=[smem, smem, vmem, vmem, vmem, vmem, pl.BlockSpec(memory_space=pl.ANY)],
+        in_specs=[smem, smem, vmem, vmem, vmem, vmem, pl.BlockSpec(memory_space=pltpu.HBM)],
         out_specs=(vmem, vmem),
         scratch_shapes=[
             pltpu.VMEM((9, rows, 3 * channels), jnp.bfloat16),
-            pltpu.VMEM((3, n, rows, packed), jnp.bfloat16),
+            pltpu.VMEM((2, n, rows, packed), jnp.bfloat16),
+            pltpu.VMEM((n, rows, packed - 128), jnp.bfloat16),
             pltpu.VMEM((2, rows, packed), jnp.bfloat16),
             pltpu.VMEM((2, rows, packed), jnp.bfloat16),
             pltpu.VMEM((2, 3 * channels, wide), jnp.bfloat16),
@@ -392,12 +419,12 @@
             pltpu.SemaphoreType.DMA((3,)),
             pltpu.SemaphoreType.DMA((2,)),
             pltpu.SemaphoreType.DMA((2,)),
-            pltpu.SemaphoreType.DMA((3, n)),
-            pltpu.SemaphoreType.DMA((3, n)),
-            pltpu.SemaphoreType.DMA((3, n)),
+            pltpu.SemaphoreType.DMA((4, n)),
+            pltpu.SemaphoreType.DMA((4, n)),
+            pltpu.SemaphoreType.DMA((4, n)),
         ],
         compiler_params=pltpu.CompilerParams(
-            collective_id=0, has_side_effects=True, vmem_limit_bytes=56 << 20
+            collective_id=0, has_side_effects=True, vmem_limit_bytes=40 << 20
         ),
     )(
         move_to,
@@ -408,6 +435,13 @@
         conv_bias.reshape(1, rows),
         conv_weight,
     )
+    return pl.pallas_call(
+        place_kernel,
+        out_shape=tuple(jax.ShapeDtypeStruct(r.shape, r.dtype) for r in results),
+        in_specs=[vmem, vmem],
+        out_specs=(vmem, vmem),
+        compiler_params=pltpu.CompilerParams(vmem_limit_bytes=8 << 20),
+    )(*results)
 
 
 def shards(latents, *rest):
@@ -415,6 +449,7 @@
         latents.shape[0] == 2
         and latents.shape[1] == 1
         and latents.shape[2] % 32 == 0
+        and latents.shape[3] % 128 == 32
         and lax.axis_size("req") > 2
         and lax.axis_size("mp") > 1
         and lax.axis_size("mp") * latents.shape[2] % 128 == 0

time: 48.6 us -> 48.2 us (level)
  Pallas kernels: 43.8 us -> 41.2 us
  local copies, waits for them, and re-layouts: 3.38 us -> 5.43 us
    pallas_call x1, Pallas kernels: 43.8 us -> 40.4 us  [shards_kernel(): pl.pallas_call(functools.partial(block_kernel, n, ring, LATENT_COLUMNS),...]
    unnamed x2 -> x12, local copies, waits for them, and re-layouts: 3.38 us -> 5.43 us
    pallas_call x0 -> x1, Pallas kernels: none -> 0.85 us  [shards_kernel(): pl.pallas_call(place_kernel, out_shape=tuple((jax.ShapeDtypeStruct(r.shap...]
where the time goes in v2:
time: 48.2 us; the launch traced here: 48 us
  Pallas kernels  41.2 us (85%)
  local copies, waits for them, and re-layouts  5.43 us (11%)
  between operations  1.3 us (3%)
    pallas_call x1, Pallas kernels, shards_kernel(): pl.pallas_call(functools.partial(block_kernel, n, ring, LATENT_COLUMNS),...  40.4 us
    unnamed x12, local copies, waits for them, and re-layouts  5.43 us

profile of v2, /device:TPU:0, one launch (start us, length us, event | category | flops | bytes accessed | tf_op | source)
XLA Modules:
  0.0 48.0 jit_solution(1210353052648595245)
XLA Ops:
  1.3 0.0 copy-start
  1.3 1.5 %copy-done = bf16[27,96,384]{2,1,0:T(8,128)(2,1)S(1)} copy-done((bf16[27,96,384]{2,1,0:T(8,128)(2,1)S(1)}, bf16[27,96,384]{2,1,0:T(8,128)(2,1)}, u32[]{:S(2)}) %copy-start) | copy-done | bytes 1990680
  2.8 0.0 copy-start.1
  2.8 1.0 %copy-done.1 = bf16[2,2,96,416]{3,2,1,0:T(8,128)(2,1)S(1)} copy-done((bf16[2,2,96,416]{3,2,1,0:T(8,128)(2,1)S(1)}, bf16[2,2,96,416]{3,2,1,0:T(8,128)(2,1)}, u32[]{:S(2)}) %copy-start.1) | copy-done | bytes 319512
  3.8 0.0 copy-start.2
  3.8 0.9 %copy-done.2 = bf16[2,1,96,416]{3,2,1,0:T(8,128)(2,1)S(1)} copy-done((bf16[2,1,96,416]{3,2,1,0:T(8,128)(2,1)S(1)}, bf16[2,1,96,416]{3,2,1,0:T(8,128)(2,1)}, u32[]{:S(2)}) %copy-start.2) | copy-done | bytes 159768
  4.8 0.0 copy-start.3
  4.8 0.7 %copy-done.3 = s32[2]{0:T(128)S(1)} copy-done((s32[2]{0:T(128)S(1)}, s32[2]{0:T(128)}, u32[]{:S(2)}) %copy-start.3) | copy-done | bytes 32
  5.4 0.0 copy-start.4
  5.4 0.7 %copy-done.4 = bf16[96]{0:T(256)(128)(2,1)S(1)} copy-done((bf16[96]{0:T(256)(128)(2,1)S(1)}, bf16[96]{0:T(256)(128)(2,1)}, u32[]{:S(2)}) %copy-start.4) | copy-done | bytes 216
  6.1 0.0 copy-start.5
  6.1 0.7 %copy-done.5 = f32[96]{0:T(128)S(1)} copy-done((f32[96]{0:T(128)S(1)}, f32[96]{0:T(128)}, u32[]{:S(2)}) %copy-start.5) | copy-done | bytes 408
  6.7 40.4 %shard_map.86 = (bf16[2,1,96,416]{3,2,1,0:T(8,128)(2,1)S(1)}, bf16[2,2,96,416]{3,2,1,0:T(8,128)(2,1)S(1)}) custom-call(s32[2]{0:T(128)S(1)} %copy-done.3, s32[1]{0:T(128)S(6)} %copy.9.counts_ref, bf16[2,1,96,416]{3,2,1,0:T(8,128)(2,1)S(1)} %copy-done.2, bf16[2,2,96,416]{3,2,1,0:T(8,128)(2,1)S(1)} %copy-done.1, bf16[1,96]{1,0:T(2,128)(2,1)S(1)} %bitcast.2, ...), custom_call_target="tpu_custom_call" | custom-call | tf_op jit(solution)/shard_map/pallas_call | solution.py:403
  47.1 0.9 %shard_map.87 = (bf16[2,1,96,416]{3,2,1,0:T(8,128)(2,1)}, bf16[2,2,96,416]{3,2,1,0:T(8,128)(2,1)}) custom-call(bf16[2,1,96,416]{3,2,1,0:T(8,128)(2,1)S(1)} %get-tuple-element.4.dec_ref, bf16[2,2,96,416]{3,2,1,0:T(8,128)(2,1)S(1)} %get-tuple-element.5.new_ref), custom_call_target="tpu_custom_call" | custom-call | tf_op jit(solution)/shard_map/pallas_call | solution.py:438
Async XLA Ops:
  1.3 1.6 %copy-start = (bf16[27,96,384]{2,1,0:T(8,128)(2,1)S(1)}, bf16[27,96,384]{2,1,0:T(8,128)(2,1)}, u32[]{:S(2)}) copy-start(bf16[27,96,384]{2,1,0:T(8,128)(2,1)} %w_ref.1) | copy-start | bytes 5971972
  2.8 1.0 %copy-start.1 = (bf16[2,2,96,416]{3,2,1,0:T(8,128)(2,1)S(1)}, bf16[2,2,96,416]{3,2,1,0:T(8,128)(2,1)}, u32[]{:S(2)}) copy-start(bf16[2,2,96,416]{3,2,1,0:T(8,128)(2,1)} %cache_ref.1) | copy-start | bytes 958468
  3.8 0.9 %copy-start.2 = (bf16[2,1,96,416]{3,2,1,0:T(8,128)(2,1)S(1)}, bf16[2,1,96,416]{3,2,1,0:T(8,128)(2,1)}, u32[]{:S(2)}) copy-start(bf16[2,1,96,416]{3,2,1,0:T(8,128)(2,1)} %lat_ref.1) | copy-start | bytes 479236
  4.8 0.7 %copy-start.3 = (s32[2]{0:T(128)S(1)}, s32[2]{0:T(128)}, u32[]{:S(2)}) copy-start(s32[2]{0:T(128)} %move_ref.1) | copy-start | bytes 28
  5.4 0.7 %copy-start.4 = (bf16[96]{0:T(256)(128)(2,1)S(1)}, bf16[96]{0:T(256)(128)(2,1)}, u32[]{:S(2)}) copy-start(bf16[96]{0:T(256)(128)(2,1)} %param.11) | copy-start | bytes 580
  6.1 0.7 %copy-start.5 = (f32[96]{0:T(128)S(1)}, f32[96]{0:T(128)}, u32[]{:S(2)}) copy-start(f32[96]{0:T(128)} %param.13) | copy-start | bytes 1156

commit v3 on v2

--- a/solution.py
+++ b/solution.py
@@ -403,8 +403,8 @@
     results = pl.pallas_call(
         functools.partial(block_kernel, n, ring, LATENT_COLUMNS),
         out_shape=(
-            jax.ShapeDtypeStruct(latents.shape, jnp.bfloat16),
-            jax.ShapeDtypeStruct(prior_frame_cache.shape, jnp.bfloat16),
+            pltpu.VMEM(latents.shape, jnp.bfloat16),
+            pltpu.VMEM(prior_frame_cache.shape, jnp.bfloat16),
         ),
         in_specs=[smem, smem, vmem, vmem, vmem, vmem, pl.BlockSpec(memory_space=pltpu.HBM)],
         out_specs=(vmem, vmem),
@@ -424,7 +424,7 @@
             pltpu.SemaphoreType.DMA((4, n)),
         ],
         compiler_params=pltpu.CompilerParams(
-            collective_id=0, has_side_effects=True, vmem_limit_bytes=40 << 20
+            collective_id=0, has_side_effects=True, vmem_limit_bytes=63 << 20
         ),
     )(
         move_to,

time: 48.2 us -> 43 us (0.89)
  local copies, waits for them, and re-layouts: 5.43 us -> 0 us
    unnamed x12 -> x0, local copies, waits for them, and re-layouts: 5.43 us -> none
where the time goes in v3:
time: 43 us; the launch traced here: 42.9 us
  Pallas kernels  41.6 us (97%)
  between operations  1.29 us (3%)
    pallas_call x1, Pallas kernels, shards_kernel(): pl.pallas_call(functools.partial(block_kernel, n, ring, LATENT_COLUMNS),...  40.7 us

profile of v3, /device:TPU:0, one launch (start us, length us, event | category | flops | bytes accessed | tf_op | source)
XLA Modules:
  0.0 42.9 jit_solution(4205835975451698963)
XLA Ops:
  1.3 40.7 %shard_map.86 = (bf16[2,1,96,416]{3,2,1,0:T(8,128)(2,1)S(1)}, bf16[2,2,96,416]{3,2,1,0:T(8,128)(2,1)S(1)}) custom-call(s32[2]{0:T(128)} %move_ref.1, s32[1]{0:T(128)S(6)} %copy.9.counts_ref, bf16[2,1,96,416]{3,2,1,0:T(8,128)(2,1)} %lat_ref.1, bf16[2,2,96,416]{3,2,1,0:T(8,128)(2,1)} %cache_ref.1, bf16[1,96]{1,0:T(2,128)(2,1)} %bitcast.2, f32[1,96]{1,0:T(1,128)} %bitcast.3, ...), custom_call_target="tpu_custom_call" | custom-call | tf_op jit(solution)/shard_map/pallas_call | solution.py:403
  42.0 0.9 %shard_map.87 = (bf16[2,1,96,416]{3,2,1,0:T(8,128)(2,1)}, bf16[2,2,96,416]{3,2,1,0:T(8,128)(2,1)}) custom-call(bf16[2,1,96,416]{3,2,1,0:T(8,128)(2,1)S(1)} %get-tuple-element.4.dec_ref, bf16[2,2,96,416]{3,2,1,0:T(8,128)(2,1)S(1)} %get-tuple-element.5.new_ref), custom_call_target="tpu_custom_call" | custom-call | tf_op jit(solution)/shard_map/pallas_call | solution.py:438

commit v4 on v3

--- a/solution.py
+++ b/solution.py
@@ -336,23 +336,40 @@
             preferred_element_type=jnp.float32,
         )
 
+    def unpack(s, src):
+        pair = gath[1, src]
+        if s == 1:
+            rest = last[src].astype(jnp.float32)
+            head = pair[:, packed - 128 :].astype(jnp.float32)
+            pair = jnp.concatenate([rest, head], axis=1)
+            pair = pltpu.roll(pair, spill, axis=1).astype(jnp.bfloat16)
+        at = pl.multiple_of(src * rows, rows)
+        stack[s, pl.ds(at, rows)] = pair[:, :wide]
+        stack[s, pl.ds(channels + at, rows)] = second_half(pair, pixels, wide)
+
+    def unpack_arrived(s, d):
+        @pl.when(me - d >= 0)
+        def _():
+            unpack(s, me - d)
+
+        @pl.when(me + d <= n - 1)
+        def _():
+            unpack(s, me + d)
+
+    unpack(0, me)
+    unpack(1, me)
     for d in range(1, n - 1):
         relay(2, d)
         relay(3, d)
+        unpack_arrived(0, d)
+        unpack_arrived(1, d)
 
     lane = lax.broadcasted_iota(jnp.int32, (1, wide), 1)
     column = lax.rem(lane, row_width)
     bias = column_of(bias_ref[...])
     for s in range(2):
         relay(2 + s, n - 1)
-        pair = gath[1].reshape(channels, packed)
-        if s == 1:
-            rest = last[...].reshape(channels, packed - 128).astype(jnp.float32)
-            head = pair[:, packed - 128 :].astype(jnp.float32)
-            pair = jnp.concatenate([rest, head], axis=1)
-            pair = pltpu.roll(pair, spill, axis=1).astype(jnp.bfloat16)
-        stack[s, :channels] = pair[:, :wide]
-        stack[s, pl.ds(channels, channels)] = second_half(pair, pixels, wide)
+        unpack_arrived(s, n - 1)
         new_ref[s, 0] = stack[s, pl.ds(channels + own, rows), :pixels]
         acc[s] += jnp.dot(
             wcat[:, :, : 2 * channels].reshape(taps, 2 * channels),

time: 43 us -> 43.1 us (level)
  no operation moved by 1% of the time
where the time goes in v4:
time: 43.1 us; the launch traced here: 42.9 us
  Pallas kernels  41.6 us (97%)
  between operations  1.29 us (3%)
    pallas_call x1, Pallas kernels, shards_kernel(): pl.pallas_call(functools.partial(block_kernel, n, ring, LATENT_COLUMNS),...  40.8 us

profile of v4, /device:TPU:0, one launch (start us, length us, event | category | flops | bytes accessed | tf_op | source)
XLA Modules:
  0.0 42.9 jit_solution(9807391004853321770)
XLA Ops:
  1.3 40.8 %shard_map.86 = (bf16[2,1,96,416]{3,2,1,0:T(8,128)(2,1)S(1)}, bf16[2,2,96,416]{3,2,1,0:T(8,128)(2,1)S(1)}) custom-call(s32[2]{0:T(128)} %move_ref.1, s32[1]{0:T(128)S(6)} %copy.9.counts_ref, bf16[2,1,96,416]{3,2,1,0:T(8,128)(2,1)} %lat_ref.1, bf16[2,2,96,416]{3,2,1,0:T(8,128)(2,1)} %cache_ref.1, bf16[1,96]{1,0:T(2,128)(2,1)} %bitcast.2, f32[1,96]{1,0:T(1,128)} %bitcast.3, ...), custom_call_target="tpu_custom_call" | custom-call | tf_op jit(solution)/shard_map/pallas_call | solution.py:420
  42.0 0.9 %shard_map.87 = (bf16[2,1,96,416]{3,2,1,0:T(8,128)(2,1)}, bf16[2,2,96,416]{3,2,1,0:T(8,128)(2,1)}) custom-call(bf16[2,1,96,416]{3,2,1,0:T(8,128)(2,1)S(1)} %get-tuple-element.4.dec_ref, bf16[2,2,96,416]{3,2,1,0:T(8,128)(2,1)S(1)} %get-tuple-element.5.new_ref), custom_call_target="tpu_custom_call" | custom-call | tf_op jit(solution)/shard_map/pallas_call | solution.py:455

commit v5 on v4

--- a/solution.py
+++ b/solution.py
@@ -247,7 +247,7 @@
         def _():
             down_copy(j, me).start()
 
-    def relay(j, d):
+    def relay_up(j, d):
         @pl.when(me - d >= 0)
         def _():
             down_copy(j, me - d).wait_recv()
@@ -256,6 +256,7 @@
             def _():
                 up_copy(j, me - d).start()
 
+    def relay_down(j, d):
         @pl.when(me + d <= n - 1)
         def _():
             up_copy(j, me + d).wait_recv()
@@ -263,6 +264,17 @@
             @pl.when(me > 0)
             def _():
                 down_copy(j, me + d).start()
+
+    def relay(j, d):
+        @pl.when(2 * me >= n)
+        def _():
+            relay_up(j, d)
+            relay_down(j, d)
+
+        @pl.when(2 * me < n)
+        def _():
+            relay_down(j, d)
+            relay_up(j, d)
 
     send_own(0)
     send_own(1)

time: 43.1 us -> 43.1 us (level)
  no operation moved by 1% of the time
where the time goes in v5:
time: 43.1 us; the launch traced here: 42.9 us
  Pallas kernels  41.6 us (97%)
  between operations  1.29 us (3%)
    pallas_call x1, Pallas kernels, shards_kernel(): pl.pallas_call(functools.partial(block_kernel, n, ring, LATENT_COLUMNS),...  40.8 us

profile of v5, /device:TPU:0, one launch (start us, length us, event | category | flops | bytes accessed | tf_op | source)
XLA Modules:
  0.0 42.9 jit_solution(12911983092147804333)
XLA Ops:
  1.3 40.8 %shard_map.86 = (bf16[2,1,96,416]{3,2,1,0:T(8,128)(2,1)S(1)}, bf16[2,2,96,416]{3,2,1,0:T(8,128)(2,1)S(1)}) custom-call(s32[2]{0:T(128)} %move_ref.1, s32[1]{0:T(128)S(6)} %copy.9.counts_ref, bf16[2,1,96,416]{3,2,1,0:T(8,128)(2,1)} %lat_ref.1, bf16[2,2,96,416]{3,2,1,0:T(8,128)(2,1)} %cache_ref.1, bf16[1,96]{1,0:T(2,128)(2,1)} %bitcast.2, f32[1,96]{1,0:T(1,128)} %bitcast.3, ...), custom_call_target="tpu_custom_call" | custom-call | tf_op jit(solution)/shard_map/pallas_call | solution.py:432
  42.0 0.9 %shard_map.87 = (bf16[2,1,96,416]{3,2,1,0:T(8,128)(2,1)}, bf16[2,2,96,416]{3,2,1,0:T(8,128)(2,1)}) custom-call(bf16[2,1,96,416]{3,2,1,0:T(8,128)(2,1)S(1)} %get-tuple-element.4.dec_ref, bf16[2,2,96,416]{3,2,1,0:T(8,128)(2,1)S(1)} %get-tuple-element.5.new_ref), custom_call_target="tpu_custom_call" | custom-call | tf_op jit(solution)/shard_map/pallas_call | solution.py:467
